TPU v7x, 32 devices: a whole 2x2x4 slice. The times are simulated.
32 devices in a mesh: seq: 8 (over z, x), dp: 4 (over y, core).
Axes of the slice: x: 2, y: 2, z: 4, core: 2. Of those that a mesh axis runs over, the one named last changes fastest.
Arguments:
- conv_input: bfloat16 [4, 2048, 2816], P('dp', 'seq'), may hold values from -6 to 6
- gate_input: bfloat16 [4, 2048, 2560], P('dp', 'seq'), may hold values from -6 to 6
- step_input: float32 [4, 40, 2048], P('dp', None, 'seq'), may hold values from -7.5 to 2048
- filter_taps: float32 [4, 2816], replicated, may hold values from -3 to 3
- filter_bias: float32 [2816], replicated, may hold values from -0.5 to 0.5
- step_bias: float32 [40], replicated, may hold values from -1 to 1
- decay_log: float32 [40], replicated, may hold values from -13 to 3
- skip_gain: float32 [40], replicated, may hold values from 0.5 to 1.5
- norm_weight: float32 [2560], replicated, may hold values from 0.5 to 1.5
- output_weight: bfloat16 [2560, 1280], P('dp'), may hold values from -0.125 to 0.125
- output_grad: bfloat16 [4, 2048, 1280], P('dp', 'seq'), may hold values from -6 to 6
Outputs:
- input_grad: bfloat16 [4, 2048, 2816], P('dp', 'seq')
- gate_grad: bfloat16 [4, 2048, 2560], P('dp', 'seq')
- step_grad: float32 [4, 40, 2048], P('dp', None, 'seq')
- weight_grad: float32 [2560, 1280], P('dp')
- filter_grads: float32 [5, 2816], replicated
- norm_grad: float32 [2560], replicated
- head_grads: float32 [3, 40], replicated
All inputs are finite; a program needn't handle non-finite values.
Results may differ from a plain program's by a relative error of at most 0.0029.
Values may be sent and summed in bfloat16 or wider, within the bound.
A program may use at most 192 MiB of HBM per device.

v0:
```python
import jax
import jax.numpy as jnp
from jax import lax
from jax.sharding import PartitionSpec as P

HEADS = 40
HEAD_DIM = 64
STATE = 128
SPAN = 256
INNER = 2560


HIGHEST = lax.Precision.HIGHEST
MASKED = -1e30
EPSILON = 1e-05


def passed_along(value, axis, steps):
    count = lax.axis_size(axis)
    first, last = (max(0, -steps), min(count, count - steps))
    return lax.ppermute(value, axis, [(source, source + steps) for source in range(first, last)])


def entering_2(value, axis, combine, identity, reverse):
    length, position = (lax.axis_size(axis), lax.axis_index(axis))
    everything = jax.tree.map(lambda part: lax.all_gather(part, axis), value)
    start = jax.tree.map(
        lambda part, zero: jnp.broadcast_to(jnp.asarray(zero, part.dtype), part.shape),
        value,
        identity,
    )

    def lap(k, before):
        at = length - 1 - k if reverse else k
        reached = at > position if reverse else at < position
        new = combine(before, jax.tree.map(lambda part: part[at], everything))
        return jax.tree.map(lambda a, b: jnp.where(reached, a, b), new, before)

    return lax.fori_loop(0, length, lap, start)


def affine(earlier, later):
    return (earlier[0] * later[0], later[0][:, None, None] * earlier[1] + later[1])


def prepare(extended, step_rows, filter_taps, filter_bias, step_bias, decay_log):
    width = filter_taps.shape[0]
    length = extended.shape[0] - width + 1
    filtered = filter_bias + filter_taps[0] * extended[0:length]
    for offset in range(1, width):
        filtered = filtered + filter_taps[offset] * extended[offset : offset + length]
    activated = jax.nn.silu(filtered)
    step_sizes = jax.nn.softplus(step_rows + step_bias[:, None])
    decay_rates = step_sizes * (-jnp.exp(decay_log))[:, None]
    blocks = length // SPAN
    cumsums = jnp.cumsum(decay_rates.reshape(HEADS, blocks, SPAN), axis=2)
    values = activated[:, :INNER].reshape(blocks, SPAN, HEADS, HEAD_DIM)
    key_side = activated[:, INNER : INNER + STATE].reshape(blocks, SPAN, STATE)
    scaled = values * step_sizes.reshape(HEADS, blocks, SPAN).transpose(1, 2, 0)[..., None]
    to_end = jnp.exp(cumsums[:, :, -1:] - cumsums)
    block_states = jnp.einsum("hcs,cshp,csn->chpn", to_end, scaled, key_side, precision=HIGHEST)
    decays = jnp.exp(cumsums[:, :, -1]).T
    return (activated, cumsums, scaled, block_states, decays)


def summarize(block_states, decays):
    product = jnp.ones((decays.shape[1],), jnp.float32)
    running = jnp.zeros(block_states.shape[1:], jnp.float32)
    running = decays[0][:, None, None] * running + block_states[0]
    product = product * decays[0]
    return (product, running)


def finish(
    activated, cumsums, scaled, block_states, decays, entering, skip_gain, gate_rows, norm_weight
):
    blocks = cumsums.shape[1]
    length = blocks * SPAN
    values = activated[:, :INNER].reshape(blocks, SPAN, HEADS, HEAD_DIM)
    key_side = activated[:, INNER : INNER + STATE].reshape(blocks, SPAN, STATE)
    query_side = activated[:, INNER + STATE :].reshape(blocks, SPAN, STATE)
    starting = []
    starting.append(entering)
    starting = jnp.stack(starting)
    scores = jnp.einsum("ctn,csn->cts", query_side, key_side, precision=HIGHEST)
    differences = cumsums[:, :, :, None] - cumsums[:, :, None, :]
    causal = jnp.tril(jnp.ones((SPAN, SPAN), dtype=bool))
    weights = scores[None] * jnp.exp(jnp.where(causal, differences, MASKED))
    inside = jnp.einsum("hcts,cshp->cthp", weights, scaled, precision=HIGHEST)
    from_state = (
        jnp.einsum("ctn,chpn->cthp", query_side, starting, precision=HIGHEST)
        * jnp.exp(cumsums).transpose(1, 2, 0)[..., None]
    )
    result = inside + from_state + skip_gain[:, None] * values
    scanned = result.reshape(length, INNER)
    gated = scanned * jax.nn.silu(gate_rows)
    inverse_rms = lax.rsqrt(jnp.mean(gated * gated, axis=1, keepdims=True) + EPSILON)
    return gated * inverse_rms * norm_weight


def body(
    conv_input,
    gate_input,
    step_input,
    filter_taps,
    filter_bias,
    step_bias,
    decay_log,
    skip_gain,
    norm_weight,
    output_weight,
    output_grad,
):
    kernel_rows = filter_taps.shape[0] - 1
    raw_rows = conv_input[0]
    before = passed_along(raw_rows[-kernel_rows:], "seq", 1)
    extended = jnp.concatenate([before, raw_rows], axis=0).astype(jnp.float32)
    gate_rows = gate_input[0].astype(jnp.float32)
    step_rows = step_input[0]
    cotangent = output_grad[0]
    tokens = cotangent.shape[0]
    primals, pull_first = jax.vjp(
        prepare, extended, step_rows, filter_taps, filter_bias, step_bias, decay_log
    )
    activated, cumsums, scaled, block_states, decays = primals
    summary, pull_summary = jax.vjp(summarize, block_states, decays)
    identity = (jnp.ones_like(summary[0]), jnp.zeros_like(summary[1]))
    _, entering = entering_2(summary, "seq", affine, identity, False)
    normed, pull_second = jax.vjp(
        finish,
        activated,
        cumsums,
        scaled,
        block_states,
        decays,
        entering,
        skip_gain,
        gate_rows,
        norm_weight,
    )
    normed_low = normed.astype(jnp.bfloat16)
    groups = lax.axis_size("dp")
    own_rows = output_weight.shape[0]
    partial_columns = lax.dot_general(
        lax.all_gather(cotangent, "dp", axis=0, tiled=True),
        output_weight,
        (((1,), (1,)), ((), ())),
        preferred_element_type=jnp.float32,
    )
    regrouped = partial_columns.reshape(groups, tokens, own_rows)
    normed_grad = lax.all_to_all(regrouped, "dp", split_axis=0, concat_axis=2, tiled=True).reshape(
        tokens, groups * own_rows
    )
    weight_piece = lax.psum_scatter(
        lax.dot_general(
            normed_low, cotangent, (((0,), (0,)), ((), ())), preferred_element_type=jnp.float32
        ),
        "dp",
        scatter_dimension=0,
        tiled=True,
    )
    weight_grad = lax.psum(weight_piece, "seq")
    second = pull_second(normed_grad)
    (
        grad_activated,
        grad_cumsums,
        grad_scaled,
        grad_states,
        grad_decays,
        grad_entering,
        grad_skip,
        grad_gate,
        grad_norm,
    ) = second
    _, end_grad = entering_2((summary[0], grad_entering), "seq", affine, identity, True)
    decay_grad = jnp.sum(end_grad * entering, axis=(1, 2))
    more_states, more_decays = pull_summary((decay_grad, end_grad))
    first = pull_first(
        (
            grad_activated,
            grad_cumsums,
            grad_scaled,
            grad_states + more_states,
            grad_decays + more_decays,
        )
    )
    grad_extended, grad_steps, grad_taps, grad_bias, grad_step_bias, grad_decay_log = first
    returned = passed_along(grad_extended[:kernel_rows], "seq", -1)
    own_part = grad_extended[kernel_rows:]
    own_part = jnp.concatenate(
        [own_part[:-kernel_rows], own_part[-kernel_rows:] + returned], axis=0
    )
    filter_part = jnp.concatenate([grad_taps, grad_bias[None]], axis=0)
    head_part = jnp.stack([grad_step_bias, grad_decay_log, grad_skip])
    filter_grads, norm_grad, head_grads = lax.psum(
        (filter_part, grad_norm, head_part), ("seq", "dp")
    )
    input_grad = own_part.astype(jnp.bfloat16)[None]
    gate_grad = grad_gate.astype(jnp.bfloat16)[None]
    step_grad = grad_steps[None]
    return (input_grad, gate_grad, step_grad, weight_grad, filter_grads, norm_grad, head_grads)


def solution(mesh):
    return jax.shard_map(
        body,
        mesh=mesh,
        in_specs=(
            P("dp", "seq", None),
            P("dp", "seq", None),
            P("dp", None, "seq"),
            P(),
            P(),
            P(),
            P(),
            P(),
            P(),
            P("dp", None),
            P("dp", "seq", None),
        ),
        out_specs=(
            P("dp", "seq", None),
            P("dp", "seq", None),
            P("dp", None, "seq"),
            P("dp", None),
            P(),
            P(),
            P(),
        ),
        check_vma=False,
    )
```

profile of v0, /device:TPU:0, one launch (start us, length us, event | category | flops | bytes accessed | tf_op | source)
XLA Modules:
  0.0 764.6 jit_solution(17478603161339498694)
XLA Ops:
  8.8 4.9 collective-permute-start
  20.2 3.0 fusion.21
  23.2 1.6 copy-done.12
  24.7 1.9 slice.95
  26.6 3.2 copy.94
  29.8 5.0 fusion.69
  34.8 3.0 all-gather.8.cloned.1.call-done
  37.9 5.5 fusion.48
  43.4 4.7 all-to-all-start
  49.6 23.0 %all-reduce.15 = f32[320]{0:T(512)S(1)} all-reduce(f32[320]{0:T(512)S(1)} %dynamic-update-slice), channel_id=3, replica_groups=mesh['seq'=8,'dp'=4] {'seq'}, use_global_device_ids=true, to_apply=%add.15 | all-reduce | flops 320 | bytes 2560
  72.7 1.8 copy.100
  74.6 1.3 fusion.98
  76.0 3.4 all-to-all-done
  79.4 3.2 copy.93
  82.6 108.7 %all-gather.10.cloned.1.call-done = f32[320,64,128]{2,1,0:T(8,128)} async-done(((f32[40,64,128]{2,1,0:T(8,128)}), f32[320,64,128]{2,1,0:T(8,128)}) %all-gather.10.cloned.1.call-update) | async-done | bytes 10485776 | tf_op jit(solution)/shard_map/all_gather | solution.py:26
  191.3 13.2 %while.30 = (s32[]{:T(128)}, f32[40,64,128]{2,1,0:T(8,128)S(1)}, s32[]{:T(128)}, f32[8,40]{1,0:T(8,128)S(1)}, f32[8,40,64,128]{3,2,1,0:T(8,128)}, /*index=5*/s32[]{:T(128)}, s32[]{:T(128)}) while((s32[]{:T(128)}, f32[40,64,128]{2,1,0:T(8,128)S(1)}, s32[]{:T(128)}, f32[8,40]{1,0:T(8,128)S(1)}, f32[8,40,64,128]{3,2,1,0:T(8,128)}, ...), condition=%wide.region_3.4_spmd.clone, body=%wide.region_2.3_spmd.clone.sunk | while | flops 1310724 | bytes 3932745 | solution.py:39
  191.3 1.6 fusion.137
  193.0 1.6 fusion.137
  194.6 1.6 fusion.137
  196.3 1.6 fusion.137
  198.0 1.6 fusion.137
  199.6 1.6 fusion.137
  201.3 1.6 fusion.137
  202.9 1.6 fusion.137
  204.6 3.3 fusion.93
  207.9 15.5 %multiply_reduce_fusion.8 = (f32[256]{0:T(256)S(1)}, f32[256]{0:T(256)S(1)}, f32[1,256,40,64]{1,3,2,0:T(8,128)S(1)}, f32[1,256,40,64]{1,3,2,0:T(8,128)}) fusion(f32[1,256,40,64]{1,3,2,0:T(8,128)} %bitcast.259, f32[40,64]{1,0:T(8,128)S(1)} %mul.591, f32[1,256,40,64]{1,3,2,0:T(8,128)} %bitcast.262, f32[1,256,40,64]{1,3,2,0:T(8,128)S(1)} %bitcast.254, ...), kind=kOutput, calls=%fused_computation.79 | convolution fusion | flops 2030960128 | bytes 18813088 | tf_op jit(solution)/shard_map/jvp(hcts,cshp->cthp)/dot_general | solution.py:89
  223.5 2.6 broadcast_multiply_fusion.5
  226.0 1.5 copy-done.9
  227.5 4.2 fusion.44
  231.8 8.5 %fusion.86 = f32[2560,1280]{1,0:T(8,128)} fusion(bf16[256,2560]{0,1:T(8,128)(2,1)S(1)} %bitcast.268, bf16[1,256,1280]{2,1,0:T(8,128)(2,1)} %param.25), kind=kOutput, calls=%fused_computation.114 | convolution fusion | flops 1677721600 | bytes 15073280 | tf_op jit(solution)/shard_map/dot_general | solution.py:155
  240.6 3.2 convert_element_type.75
  243.8 3.7 copy.129
  247.6 15.7 %fusion.8 = (f32[40,256]{1,0:T(8,128)S(1)}, f32[40,256]{1,0:T(8,128)}, f32[256,256]{1,0:T(8,128)S(1)}) fusion(f32[40,256]{1,0:T(8,128)S(1)} %get-tuple-element.347, f32[256,256]{1,0:T(8,128)S(1)} %copy-done.19, pred[256,256]{1,0:T(8,128)(4,1)S(1)} %iota_compare_fusion, f32[256,40,64]{0,2,1:T(8,128)S(1)} %bitcast.256, f32[256,40]{0,1:T(8,128)S(1)} %fusion.106, ...), kind=kOutput, calls=%fused_computation.13 | convolution fusion | flops 2037428224 | bytes 5996544 | tf_op jit(solution)/shard_map/transpose(jvp(hcts,cshp->cthp))/dot_general | solution.py:89
  263.2 3.2 copy.101
  266.4 3.2 copy.117
  269.6 4.3 fusion.33
  274.6 3.3 copy.106
  277.8 1.6 fusion.101
  279.5 6.0 fusion.83
  286.8 3.2 fusion.29
  290.0 90.6 %all-gather.12.cloned.1.call-done = f32[320,64,128]{2,1,0:T(8,128)} async-done(((f32[40,64,128]{2,1,0:T(8,128)}), f32[320,64,128]{2,1,0:T(8,128)}) %all-gather.12.cloned.1.call-update) | async-done | bytes 10485776 | tf_op jit(solution)/shard_map/all_gather | solution.py:26
  380.6 20.8 %while.31 = (s32[]{:T(128)}, f32[40,64,128]{2,1,0:T(8,128)S(1)}, s32[]{:T(128)}, f32[8,40]{1,0:T(8,128)}, f32[8,40,64,128]{3,2,1,0:T(8,128)}, /*index=5*/s32[]{:T(128)}, s32[]{:T(128)}, s32[]{:T(128)}, s32[]{:T(128)}) while((s32[]{:T(128)}, f32[40,64,128]{2,1,0:T(8,128)S(1)}, s32[]{:T(128)}, f32[8,40]{1,0:T(8,128)}, ...), condition=%wide.region_8.9_spmd.clone, body=%wide.region_7.8_spmd.clone.sunk | while | flops 1310728 | bytes 3932807 | solution.py:39
  381.3 1.6 fusion.138
  383.6 1.6 fusion.138
  386.0 2.0 fusion.138
  388.7 1.7 fusion.138
  391.1 2.1 fusion.138
  393.9 2.1 fusion.138
  396.7 2.1 fusion.138
  399.5 1.7 fusion.138
  401.9 5.6 fusion.39
  408.5 2.5 reduce-window.16
  411.3 12.6 %multiply_reduce_fusion.5 = (f32[40]{0:T(128)S(1)}, f32[256,40]{0,1:T(8,128)S(1)}, f32[1,256,40,64]{1,3,2,0:T(8,128)}) fusion(f32[1,256,40,64]{1,3,2,0:T(8,128)} %copy-done.9, f32[1,256,40,64]{1,3,2,0:T(8,128)} %bitcast.252, f32[256,40]{0,1:T(8,128)S(1)} %fusion.106, f32[256,40]{0,1:T(8,128)S(1)} %get-tuple-element.346, ...), kind=kOutput, calls=%fused_computation.75 | convolution fusion | flops 2025707520 | bytes 10977440 | tf_op jit(solution)/shard_map/transpose(jvp(hcts,cshp->cthp))/dot_general | solution.py:89
  423.9 3.4 copy.103
  427.4 6.1 fusion.80
  433.5 6.0 multiply_reduce_fusion.4
  441.4 4.4 fusion.26
  445.8 38.6 %reduce-scatter.2.cloned.1.call-done = f32[640,1280]{1,0:T(8,128)} async-done(((f32[2560,1280]{1,0:T(8,128)}), f32[640,1280]{1,0:T(8,128)}) %reduce-scatter.2.cloned.1.call-update) | async-done | bytes 3276816 | tf_op jit(solution)/shard_map/reduce_scatter | solution.py:154
  484.4 2.7 broadcast_multiply_fusion.3
  487.2 1.3 collective-permute-start.1
  490.7 2.4 collective-permute-done.1
  494.3 120.0 %all-reduce.22.cloned.1.call-done = (f32[5,2816]{1,0:T(8,128)}, f32[2560]{0:T(1024)}, f32[3,40]{1,0:T(4,128)}) async-done(((f32[5,2816]{1,0:T(8,128)}, f32[2560]{0:T(1024)}, f32[3,40]{1,0:T(4,128)}), (f32[5,2816]{1,0:T(8,128)}, f32[2560]{0:T(1024)}, f32[3,40]{1,0:T(4,128)})) %all-reduce.22.cloned.1.call-update) | async-done | bytes 67056 | tf_op jit(solution)/shard_map/psum | solution.py:195
  614.4 137.1 %all-reduce.20.cloned.1.call-done = f32[640,1280]{1,0:T(8,128)} async-done(((f32[640,1280]{1,0:T(8,128)}), f32[640,1280]{1,0:T(8,128)}) %all-reduce.20.cloned.1.call-update) | async-done | bytes 3276816 | tf_op jit(solution)/shard_map/psum | solution.py:162
  751.5 4.0 copy.175
  (158 shorter events, 25.9 us)
Async XLA Ops:
  7.2 30.7 %copy-start = (bf16[640,1280]{1,0:T(8,128)(2,1)S(1)}, bf16[640,1280]{1,0:T(8,128)(2,1)}, u32[]{:S(2)}) copy-start(bf16[640,1280]{1,0:T(8,128)(2,1)} %param.24) | copy-start | bytes 4915204
  7.2 12.7 %copy-start.16 = (bf16[1,256,2816]{2,1,0:T(8,128)(2,1)S(1)}, bf16[1,256,2816]{2,1,0:T(8,128)(2,1)}, u32[]{:S(2)}) copy-start(bf16[1,256,2816]{2,1,0:T(8,128)(2,1)} %param.15) | copy-start | bytes 4325380
  7.2 30.7 %all-gather.8.cloned.1.call-start = ((), (), s32[]{:S(2)}) async-start(), calls=%async_computation.4 | async-start | bytes 3276800 | tf_op jit(solution)/shard_map/all_gather | solution.py:145
  7.9 183.4 %all-gather.10.cloned.1.call-start = ((), (), s32[]{:S(2)}) async-start(), calls=%async_computation.5 | async-start | bytes 11796480 | tf_op jit(solution)/shard_map/all_gather | solution.py:26
  8.8 11.1 %collective-permute-start = (bf16[3,2816]{1,0:T(4,128)(2,1)S(1)}, bf16[3,2816]{1,0:T(4,128)(2,1)S(1)}, u32[]{:S(2)}, u32[]{:S(2)}) collective-permute-start(bf16[3,2816]{1,0:T(4,128)(2,1)S(1)} %slice_bitcast_fusion), channel_id=1, source_target_pairs={{0,4},{4,8},{8,12},{12,16},{16,20},{20,24},{24,28},{1,5},{5,9},{9,... | collective-permute-start | bytes 50696 | tf_op jit(solution)/shard_map/ppermute | solution.py:21
  16.5 3.7 copy-start.24
  20.2 3.0 copy-start.2
  23.2 1.6 copy-start.12
  43.4 4.8 copy-start.31
  43.4 29.3 %copy-start.13 = (bf16[1,256,2560]{2,1,0:T(8,128)(2,1)S(1)}, bf16[1,256,2560]{2,1,0:T(8,128)(2,1)}, u32[]{:S(2)}) copy-start(bf16[1,256,2560]{2,1,0:T(8,128)(2,1)} %param.16) | copy-start | bytes 3932164
  43.4 36.0 %all-to-all-start = ((f32[4,256,640]{2,1,0:T(8,128)}), f32[4,256,640]{2,1,0:T(8,128)}, u32[]{:S(2)}, u32[]{:S(2)}) async-start(f32[4,256,640]{2,1,0:T(8,128)} %bitcast.271), calls=%async_computation | async-start | bytes 5242880 | tf_op jit(solution)/shard_map/all_to_all | solution.py:151
  48.0 26.5 %copy-start.22 = (f32[2560]{0:T(1024)S(1)}, f32[2560]{0:T(1024)}, u32[]{:S(2)}) copy-start(f32[2560]{0:T(1024)} %param.23) | copy-start | bytes 30724
  48.0 332.5 %all-gather.12.cloned.1.call-start = ((), (), s32[]{:S(2)}) async-start(), calls=%async_computation.6 | async-start | bytes 11796480 | tf_op jit(solution)/shard_map/all_gather | solution.py:26
  76.0 131.9 %copy-start.18 = (f32[256,256]{1,0:T(8,128)}, f32[256,256]{1,0:T(8,128)S(1)}, u32[]{:S(2)}) copy-start(f32[256,256]{1,0:T(8,128)S(1)} %fusion.98) | copy-start | bytes 786436
  204.6 18.9 %copy-start.27 = (f32[8,40]{1,0:T(8,128)}, f32[8,40]{1,0:T(8,128)S(1)}, u32[]{:S(2)}) copy-start(f32[8,40]{1,0:T(8,128)S(1)} %get-tuple-element.516) | copy-start | bytes 3844
  204.6 3.3 copy-start.4
  204.6 3.3 copy-start.29
  207.9 15.6 %copy-start.15 = (f32[256,40,64]{0,2,1:T(8,128)}, f32[256,40,64]{0,2,1:T(8,128)S(1)}, u32[]{:S(2)}) copy-start(f32[256,40,64]{0,2,1:T(8,128)S(1)} %fusion.93) | copy-start | bytes 7864324
  207.9 15.6 %copy-start.7 = (f32[1,256,4,640]{1,3,2,0:T(8,128)S(1)}, f32[1,256,4,640]{1,3,2,0:T(8,128)}, u32[]{:S(2)}) copy-start(f32[1,256,4,640]{1,3,2,0:T(8,128)} %copy.93) | copy-start | bytes 7864324
  207.9 15.6 %copy-start.11 = (f32[1,256,2560]{1,2,0:T(8,128)S(1)}, f32[1,256,2560]{1,2,0:T(8,128)}, u32[]{:S(2)}) copy-start(f32[1,256,2560]{1,2,0:T(8,128)} %copy.100) | copy-start | bytes 7864324
  226.0 1.5 copy-start.9
  231.7 252.6 %reduce-scatter.2.cloned.1.call-start = ((), (), s32[]{:S(2)}) async-start(), calls=%async_computation.2 | async-start | bytes 16384000 | tf_op jit(solution)/shard_map/reduce_scatter | solution.py:154
  240.3 374.0 %all-reduce.22.cloned.1.call-start = ((), (), s32[]{:S(2)}) async-start(), calls=%async_computation.7 | async-start | bytes 208896 | tf_op jit(solution)/shard_map/psum | solution.py:195
  240.6 7.0 copy-start.19
  243.8 3.8 copy-start.5
  243.8 3.8 copy-start.10
  277.8 8.9 %copy-start.6 = (f32[1,256,40,64]{1,3,2,0:T(8,128)S(1)}, f32[1,256,40,64]{1,3,2,0:T(8,128)}, u32[]{:S(2)}) copy-start(f32[1,256,40,64]{1,3,2,0:T(8,128)} %get-tuple-element.358) | copy-start | bytes 7864324
  277.8 8.9 %copy-start.8 = (f32[1,256,4,640]{1,3,2,0:T(8,128)S(1)}, f32[1,256,4,640]{1,3,2,0:T(8,128)}, u32[]{:S(2)}) copy-start(f32[1,256,4,640]{1,3,2,0:T(8,128)} %copy.93) | copy-start | bytes 7864324
  401.9 6.4 copy-start.23
  401.9 9.4 %copy-start.20 = (f32[256,256]{1,0:T(8,128)S(1)}, f32[256,256]{1,0:T(8,128)}, u32[]{:S(2)}) copy-start(f32[256,256]{1,0:T(8,128)} %copy-done.18) | copy-start | bytes 786436
  427.3 6.1 copy-start.3
  433.5 6.2 copy-start.17
  433.5 6.2 copy-start.26
  433.5 6.4 copy-start.30
  433.5 7.8 %copy-start.14 = (bf16[1,256,2560]{2,1,0:T(8,128)(2,1)S(1)}, bf16[1,256,2560]{2,1,0:T(8,128)(2,1)}, u32[]{:S(2)}) copy-start(bf16[1,256,2560]{2,1,0:T(8,128)(2,1)} %param.16) | copy-start | bytes 3932164
  441.3 310.2 %all-reduce.20.cloned.1.call-start = ((), (), s32[]{:S(2)}) async-start(), calls=%async_computation.3 | async-start | bytes 6553600 | tf_op jit(solution)/shard_map/psum | solution.py:162
  487.2 5.9 collective-permute-start.1
  751.5 5.8 copy-start.1
  751.5 4.0 copy-start.21
  751.5 4.6 copy-start.25
  751.5 5.2 copy-start.28
Sparse Core Ops, SparseCore 0:
  9.6 28.2 all-gather.7
  40.6 150.6 all-gather.9
  231.9 148.6 all-gather.11
  383.0 101.2 reduce-scatter.1
  490.7 123.6 all-reduce.21
  617.9 133.5 all-reduce.19
where the time goes:
time: 772 us; the launch traced here: 765 us
  waiting for transfers between devices  504 us (65%)
  matrix products  92.2 us (12%)
  other arithmetic  69.3 us (9%)
  local copies, waits for them, and re-layouts  47.9 us (6%)
  blocking collectives  23 us (3%)
  between operations  15.9 us (2%)
  starting transfers between devices  11.2 us (1%)
    all_gather x2, waiting for transfers between devices, entering_2(): everything = jax.tree.map(lambda part: lax.all_gather(part, axis), value)  199 us
    psum x1, waiting for transfers between devices, body(): weight_grad = lax.psum(weight_piece, 'seq')  137 us
    psum x1, waiting for transfers between devices, body(): lax.psum((filter_part, grad_norm, head_part), ('seq', 'dp'))  120 us
    dot_general x3, matrix products, finish(): inside = jnp.einsum('hcts,cshp->cthp', weights, scaled, precision=HIGHEST)  43.8 us
    reduce_scatter x1, waiting for transfers between devices, body(): lax.psum_scatter(lax.dot_general(normed_low, cotangent, (((0,), (0,)), ((...  38.6 us
    select_n x16, other arithmetic, lap(): return jax.tree.map(lambda a, b: jnp.where(reached, a, b), new, before)  27.8 us
    unnamed x1, blocking collectives  23 us
    dot_general x3, matrix products, prepare(): jnp.einsum('hcs,cshp,csn->chpn', to_end, scaled, key_side, precision=HIGH...  16.7 us
  transfers between devices with their start and end apart: 9, of which 8 were waited for; matrix products, arithmetic and copies ran while one was open for 21% of the time, Pallas kernels for 0%

commit v1 on v0

--- a/solution.py
+++ b/solution.py
@@ -10,7 +10,7 @@
 INNER = 2560
 
 
-HIGHEST = lax.Precision.HIGHEST
+PRECISE = lax.Precision.HIGH
 MASKED = -1e30
 EPSILON = 1e-05
 
@@ -21,26 +21,45 @@
     return lax.ppermute(value, axis, [(source, source + steps) for source in range(first, last)])
 
 
-def entering_2(value, axis, combine, identity, reverse):
-    length, position = (lax.axis_size(axis), lax.axis_index(axis))
-    everything = jax.tree.map(lambda part: lax.all_gather(part, axis), value)
-    start = jax.tree.map(
-        lambda part, zero: jnp.broadcast_to(jnp.asarray(zero, part.dtype), part.shape),
-        value,
-        identity,
-    )
-
-    def lap(k, before):
-        at = length - 1 - k if reverse else k
-        reached = at > position if reverse else at < position
-        new = combine(before, jax.tree.map(lambda part: part[at], everything))
-        return jax.tree.map(lambda a, b: jnp.where(reached, a, b), new, before)
-
-    return lax.fori_loop(0, length, lap, start)
-
-
-def affine(earlier, later):
-    return (earlier[0] * later[0], later[0][:, None, None] * earlier[1] + later[1])
+def spread(table, axis):
+    count = lax.axis_size(axis)
+    return lax.all_to_all(
+        jnp.broadcast_to(table[None], (count,) + table.shape),
+        axis,
+        split_axis=0,
+        concat_axis=0,
+        tiled=True,
+    )
+
+
+def carried(states, decay_table, axis, reverse):
+    count = lax.axis_size(axis)
+    heads, features, width = states.shape
+    pieces = states.reshape(heads, count, features // count, width).transpose(1, 0, 2, 3)
+    pieces = lax.all_to_all(pieces, axis, split_axis=0, concat_axis=0, tiled=True)
+    running = jnp.zeros(pieces.shape[1:], jnp.float32)
+    found = [None] * count
+    for at in reversed(range(count)) if reverse else range(count):
+        found[at] = running
+        running = decay_table[at][:, None, None] * running + pieces[at]
+    back = lax.all_to_all(jnp.stack(found), axis, split_axis=0, concat_axis=0, tiled=True)
+    return back.transpose(1, 0, 2, 3).reshape(heads, features, width)
+
+
+def summed_everywhere(parts, axes):
+    count = 1
+    for axis in axes:
+        count = count * lax.axis_size(axis)
+    flat = jnp.concatenate([part.reshape(-1) for part in parts])
+    chunk = -(-flat.shape[0] // (count * 128)) * 128
+    padded = jnp.pad(flat, (0, chunk * count - flat.shape[0])).reshape(count, chunk)
+    terms = lax.all_to_all(padded, axes, split_axis=0, concat_axis=0, tiled=True)
+    total = lax.all_gather(jnp.sum(terms, axis=0), axes, axis=0, tiled=True)
+    results, start = [], 0
+    for part in parts:
+        results.append(total[start : start + part.size].reshape(part.shape))
+        start += part.size
+    return results
 
 
 def prepare(extended, step_rows, filter_taps, filter_bias, step_bias, decay_log):
@@ -58,17 +77,9 @@
     key_side = activated[:, INNER : INNER + STATE].reshape(blocks, SPAN, STATE)
     scaled = values * step_sizes.reshape(HEADS, blocks, SPAN).transpose(1, 2, 0)[..., None]
     to_end = jnp.exp(cumsums[:, :, -1:] - cumsums)
-    block_states = jnp.einsum("hcs,cshp,csn->chpn", to_end, scaled, key_side, precision=HIGHEST)
+    block_states = jnp.einsum("hcs,cshp,csn->chpn", to_end, scaled, key_side, precision=PRECISE)
     decays = jnp.exp(cumsums[:, :, -1]).T
     return (activated, cumsums, scaled, block_states, decays)
-
-
-def summarize(block_states, decays):
-    product = jnp.ones((decays.shape[1],), jnp.float32)
-    running = jnp.zeros(block_states.shape[1:], jnp.float32)
-    running = decays[0][:, None, None] * running + block_states[0]
-    product = product * decays[0]
-    return (product, running)
 
 
 def finish(
@@ -82,13 +93,13 @@
     starting = []
     starting.append(entering)
     starting = jnp.stack(starting)
-    scores = jnp.einsum("ctn,csn->cts", query_side, key_side, precision=HIGHEST)
+    scores = jnp.einsum("ctn,csn->cts", query_side, key_side, precision=PRECISE)
     differences = cumsums[:, :, :, None] - cumsums[:, :, None, :]
     causal = jnp.tril(jnp.ones((SPAN, SPAN), dtype=bool))
     weights = scores[None] * jnp.exp(jnp.where(causal, differences, MASKED))
-    inside = jnp.einsum("hcts,cshp->cthp", weights, scaled, precision=HIGHEST)
+    inside = jnp.einsum("hcts,cshp->cthp", weights, scaled, precision=PRECISE)
     from_state = (
-        jnp.einsum("ctn,chpn->cthp", query_side, starting, precision=HIGHEST)
+        jnp.einsum("ctn,chpn->cthp", query_side, starting, precision=PRECISE)
         * jnp.exp(cumsums).transpose(1, 2, 0)[..., None]
     )
     result = inside + from_state + skip_gain[:, None] * values
@@ -123,9 +134,8 @@
         prepare, extended, step_rows, filter_taps, filter_bias, step_bias, decay_log
     )
     activated, cumsums, scaled, block_states, decays = primals
-    summary, pull_summary = jax.vjp(summarize, block_states, decays)
-    identity = (jnp.ones_like(summary[0]), jnp.zeros_like(summary[1]))
-    _, entering = entering_2(summary, "seq", affine, identity, False)
+    decay_table = spread(decays[0], "seq")
+    entering = carried(block_states[0], decay_table, "seq", False)
     normed, pull_second = jax.vjp(
         finish,
         activated,
@@ -141,25 +151,28 @@
     normed_low = normed.astype(jnp.bfloat16)
     groups = lax.axis_size("dp")
     own_rows = output_weight.shape[0]
+    everyone = lax.all_gather(cotangent, "dp", axis=0, tiled=True)
     partial_columns = lax.dot_general(
-        lax.all_gather(cotangent, "dp", axis=0, tiled=True),
-        output_weight,
-        (((1,), (1,)), ((), ())),
-        preferred_element_type=jnp.float32,
+        everyone, output_weight, (((1,), (1,)), ((), ())), preferred_element_type=jnp.float32
     )
     regrouped = partial_columns.reshape(groups, tokens, own_rows)
     normed_grad = lax.all_to_all(regrouped, "dp", split_axis=0, concat_axis=2, tiled=True).reshape(
         tokens, groups * own_rows
     )
-    weight_piece = lax.psum_scatter(
-        lax.dot_general(
-            normed_low, cotangent, (((0,), (0,)), ((), ())), preferred_element_type=jnp.float32
-        ),
-        "dp",
-        scatter_dimension=0,
+    own_columns = lax.all_to_all(normed_low, "dp", split_axis=1, concat_axis=0, tiled=True)
+    weight_piece = lax.dot_general(
+        own_columns, everyone, (((0,), (0,)), ((), ())), preferred_element_type=jnp.float32
+    )
+    spans = lax.axis_size("seq")
+    weight_terms = lax.all_to_all(
+        weight_piece.astype(jnp.bfloat16).reshape(spans, own_rows // spans, -1),
+        "seq",
+        split_axis=0,
+        concat_axis=0,
         tiled=True,
     )
-    weight_grad = lax.psum(weight_piece, "seq")
+    weight_rows = jnp.sum(weight_terms.astype(jnp.float32), axis=0)
+    weight_grad = lax.all_gather(weight_rows, "seq", axis=0, tiled=True)
     second = pull_second(normed_grad)
     (
         grad_activated,
@@ -172,16 +185,15 @@
         grad_gate,
         grad_norm,
     ) = second
-    _, end_grad = entering_2((summary[0], grad_entering), "seq", affine, identity, True)
+    end_grad = carried(grad_entering, decay_table, "seq", True)
     decay_grad = jnp.sum(end_grad * entering, axis=(1, 2))
-    more_states, more_decays = pull_summary((decay_grad, end_grad))
     first = pull_first(
         (
             grad_activated,
             grad_cumsums,
             grad_scaled,
-            grad_states + more_states,
-            grad_decays + more_decays,
+            grad_states + end_grad[None],
+            grad_decays + decay_grad[None],
         )
     )
     grad_extended, grad_steps, grad_taps, grad_bias, grad_step_bias, grad_decay_log = first
@@ -192,7 +204,7 @@
     )
     filter_part = jnp.concatenate([grad_taps, grad_bias[None]], axis=0)
     head_part = jnp.stack([grad_step_bias, grad_decay_log, grad_skip])
-    filter_grads, norm_grad, head_grads = lax.psum(
+    filter_grads, norm_grad, head_grads = summed_everywhere(
         (filter_part, grad_norm, head_part), ("seq", "dp")
     )
     input_grad = own_part.astype(jnp.bfloat16)[None]

time: 772 us -> 418 us (0.54)
  waiting for transfers between devices: 504 us -> 120 us
  starting transfers between devices: 11.2 us -> 47.2 us
  matrix products: 92.2 us -> 64.5 us
  blocking collectives: 23 us -> 40 us
    psum x2 -> x0, waiting for transfers between devices: 257 us -> none  [the longest x1 137 us: body(): weight_grad = lax.psum(weight_piece, 'seq')]
    all_gather x3 -> x2, waiting for transfers between devices: 202 us -> 0.02 us  [the longest x1 0.02 us: body(): everyone = lax.all_gather(cotangent, 'dp', axis=0, tiled=True)]
    all_to_all x0 -> x8, waiting for transfers between devices: none -> 95.5 us  [the longest x2 48.4 us: carried(): lax.all_to_all(pieces, axis, split_axis=0, concat_axis=0, tiled=True)]
    all_gather x0 -> x1, blocking collectives: none -> 40 us  [summed_everywhere(): total = lax.all_gather(jnp.sum(terms, axis=0), axes, axis=0, tiled=True)]
    reduce_scatter x1 -> x0, waiting for transfers between devices: 38.6 us -> none  [body(): lax.psum_scatter(lax.dot_general(normed_low, cotangent, (((0,), (0,)), ((...]
    all_to_all x0 -> x8, starting transfers between devices: none -> 36.9 us  [the longest x2 10.3 us: carried(): lax.all_to_all(pieces, axis, split_axis=0, concat_axis=0, tiled=True)]
    select_n x16 -> x0, other arithmetic: 27.8 us -> none  [lap(): return jax.tree.map(lambda a, b: jnp.where(reached, a, b), new, before)]
    dot_general x14, matrix products: 92.2 us -> 64.5 us  [the longest x3 30.7 us: finish(): inside = jnp.einsum('hcts,cshp->cthp', weights, scaled, precision=PRECISE)]
  transfers between devices with their start and end apart: 9 -> 13, of which waited for: 8 -> 7; matrix products, arithmetic and copies ran while one was open for 21% -> 40% of each run, Pallas kernels for 0% -> 0%
where the time goes in v1:
time: 418 us; the launch traced here: 411 us
  waiting for transfers between devices  120 us (29%)
  other arithmetic  69.1 us (17%)
  matrix products  64.5 us (15%)
  local copies, waits for them, and re-layouts  54.6 us (13%)
  starting transfers between devices  47.2 us (11%)
  blocking collectives  40 us (10%)
  between operations  15.1 us (4%)
    all_to_all x2, waiting for transfers between devices, carried(): lax.all_to_all(pieces, axis, split_axis=0, concat_axis=0, tiled=True)  48.4 us
    all_gather x1, blocking collectives, summed_everywhere(): total = lax.all_gather(jnp.sum(terms, axis=0), axes, axis=0, tiled=True)  40 us
    dot_general x3, matrix products, finish(): inside = jnp.einsum('hcts,cshp->cthp', weights, scaled, precision=PRECISE)  30.7 us
    all_to_all x2, waiting for transfers between devices, carried(): lax.all_to_all(jnp.stack(found), axis, split_axis=0, concat_axis=0, tiled...  25.8 us
    all_to_all x1, waiting for transfers between devices, body(): lax.all_to_all(regrouped, 'dp', split_axis=0, concat_axis=2, tiled=True)  20.4 us
    unnamed x113, local copies, waits for them, and re-layouts  17.5 us
    all_to_all x1, waiting for transfers between devices, body(): lax.all_to_all(weight_piece.astype(jnp.bfloat16).reshape(spans, own_rows...  13.1 us
    unnamed x10, other arithmetic  12.2 us
  transfers between devices with their start and end apart: 13, of which 7 were waited for; matrix products, arithmetic and copies ran while one was open for 40% of the time, Pallas kernels for 0%

profile of v1, /device:TPU:0, one launch (start us, length us, event | category | flops | bytes accessed | tf_op | source)
XLA Modules:
  0.0 410.9 jit_solution(12304909783855509701)
XLA Ops:
  8.1 4.9 %collective-permute-start = (bf16[3,2816]{1,0:T(4,128)(2,1)S(1)}, bf16[3,2816]{1,0:T(4,128)(2,1)S(1)}, u32[]{:S(2)}, u32[]{:S(2)}) collective-permute-start(bf16[3,2816]{1,0:T(4,128)(2,1)S(1)} %slice_bitcast_fusion), channel_id=1, source_target_pairs={{0,4},{4,8},{8,12},{12,16},{16,20},{20,24},{24,28},{1,5},{5,9},{9,... | collective-permute-start | bytes 50696 | tf_op jit(solution)/shard_map/ppermute | solution.py:21
  16.9 4.9 %all-to-all-start.1 = ((f32[8,1,40]{2,1,0:T(1,128)}), f32[8,1,40]{2,1,0:T(1,128)S(1)}, u32[]{:S(2)}, u32[]{:S(2)}) async-start(f32[8,1,40]{2,1,0:T(1,128)} %broadcast_in_dim.32), calls=%async_computation.1 | async-start | bytes 8192 | tf_op jit(solution)/shard_map/all_to_all | solution.py:26
  24.9 1.7 maximum_convert_fusion
  26.6 3.0 fusion.19
  29.6 1.6 copy-done.12
  31.2 1.9 slice.222
  33.1 3.2 copy.219
  36.4 3.0 fusion.64
  41.1 6.0 %all-to-all-start.2 = ((f32[8,40,8,128]{3,2,1,0:T(8,128)}), f32[8,40,8,128]{3,2,1,0:T(8,128)S(1)}, u32[]{:S(2)}, u32[]{:S(2)}) async-start(f32[8,40,8,128]{3,2,1,0:T(8,128)} %copy.225), calls=%async_computation.2 | async-start | bytes 2621440 | tf_op jit(solution)/shard_map/all_to_all | solution.py:39
  48.5 1.3 fusion.134
  49.9 28.0 %all-to-all-done.2 = f32[8,40,8,128]{3,2,1,0:T(8,128)S(1)} async-done(((f32[8,40,8,128]{3,2,1,0:T(8,128)}), f32[8,40,8,128]{3,2,1,0:T(8,128)S(1)}, u32[]{:S(2)}, u32[]{:S(2)}) %all-to-all-start.2) | async-done | bytes 1310752 | tf_op jit(solution)/shard_map/all_to_all | solution.py:39
  83.4 3.6 all-to-all-start.3
  87.1 5.5 %fusion.44 = f32[1024,640]{1,0:T(8,128)} fusion(bf16[640,1280]{1,0:T(8,128)(2,1)S(1)} %copy-done, bf16[1,1024,1280]{2,1,0:T(8,128)(2,1)} %all-gather.7.cloned.1.call-done), kind=kOutput, calls=%fused_computation.67 | convolution fusion | flops 1677721600 | bytes 6881280 | tf_op jit(solution)/shard_map/dot_general | solution.py:155
  92.6 25.8 %all-to-all-done.3 = f32[8,40,8,128]{3,2,1,0:T(8,128)S(1)} async-done(((f32[8,40,8,128]{3,2,1,0:T(8,128)}), f32[8,40,8,128]{3,2,1,0:T(8,128)S(1)}, u32[]{:S(2)}, u32[]{:S(2)}) %all-to-all-start.3) | async-done | bytes 1310752 | tf_op jit(solution)/shard_map/all_to_all | solution.py:45
  119.5 4.1 %all-to-all-start = ((f32[4,256,640]{2,1,0:T(8,128)}), f32[4,256,640]{2,1,0:T(8,128)S(1)}, u32[]{:S(2)}, u32[]{:S(2)}) async-start(f32[4,256,640]{2,1,0:T(8,128)} %bitcast.338), calls=%async_computation | async-start | bytes 5242880 | tf_op jit(solution)/shard_map/all_to_all | solution.py:159
  123.8 2.4 copy.229
  126.2 3.2 convert_element_type.89
  130.7 3.7 fusion.74
  134.4 20.4 %all-to-all-done = f32[4,256,640]{2,1,0:T(8,128)S(1)} async-done(((f32[4,256,640]{2,1,0:T(8,128)}), f32[4,256,640]{2,1,0:T(8,128)S(1)}, u32[]{:S(2)}, u32[]{:S(2)}) %all-to-all-start) | async-done | bytes 2621472 | tf_op jit(solution)/shard_map/all_to_all | solution.py:159
  154.8 2.5 copy.218
  157.3 10.1 %multiply_reduce_fusion.9 = (f32[256]{0:T(256)S(1)}, f32[256]{0:T(256)S(1)}, f32[1,256,40,64]{1,3,2,0:T(8,128)S(1)}) fusion(f32[1,256,40,64]{1,3,2,0:T(8,128)} %bitcast.317, f32[1,256,40,64]{1,3,2,0:T(8,128)} %bitcast.329, f32[40,64]{1,0:T(8,128)S(1)} %mul.692, f32[1,256,40,64]{1,3,2,0:T(8,128)} %bitcast.323, f32[40]{0:T(128)S(1)} %copy-done.51, ...), kind=kOutput, calls=%fused_computation.74 | convolution fusion | flops 1024327168 | bytes 16191648 | tf_op jit(solution)/shard_map/jvp(hcts,cshp->cthp)/dot_general | solution.py:100
  167.5 1.9 multiply_convert_fusion
  169.4 4.3 %all-to-all-start.6 = ((bf16[256,4,640]{0,2,1:T(8,128)(2,1)}), bf16[256,4,640]{0,2,1:T(8,128)(2,1)}, u32[]{:S(2)}, u32[]{:S(2)}) async-start(bf16[256,4,640]{0,2,1:T(8,128)(2,1)} %multiply_convert_fusion), calls=%async_computation.6 | async-start | bytes 2621440 | tf_op jit(solution)/shard_map/all_to_all | solution.py:162
  173.7 4.2 %broadcast_multiply_fusion.5 = (f32[1,256,40,64]{1,3,2,0:T(8,128)}, f32[1,256,40,64]{1,3,2,0:T(8,128)S(1)}) fusion(f32[40]{0:T(128)S(1)} %copy-done.51, f32[256]{0:T(256)S(1)} %get-tuple-element.107, f32[1,256,40,64]{1,3,2,0:T(8,128)S(1)} %get-tuple-element.108, f32[1,256,40,64]{1,3,2,0:T(8,128)} %bitcast.318, f32[256]{0:T(256)S(1)} %get-tuple-element.106, ...), kind=kLoop, calls=%fused_computation.104 | loop fusion | flops 7864320 | bytes 13119648 | tf_op jit(solution)/shard_map/transpose(jvp())/mul | solution.py:105
  177.9 1.6 copy-done.7
  179.5 2.1 fusion.67
  182.7 8.2 %all-to-all-done.6 = bf16[256,4,640]{0,2,1:T(8,128)(2,1)} async-done(((bf16[256,4,640]{0,2,1:T(8,128)(2,1)}), bf16[256,4,640]{0,2,1:T(8,128)(2,1)}, u32[]{:S(2)}, u32[]{:S(2)}) %all-to-all-start.6) | async-done | bytes 1310752 | tf_op jit(solution)/shard_map/all_to_all | solution.py:162
  191.0 4.3 %all-to-all-start.4 = ((f32[8,40,8,128]{3,2,1,0:T(8,128)}), f32[8,40,8,128]{3,2,1,0:T(8,128)}, u32[]{:S(2)}, u32[]{:S(2)}) async-start(f32[8,40,8,128]{3,2,1,0:T(8,128)} %copy.232), calls=%async_computation.4 | async-start | bytes 2621440 | tf_op jit(solution)/shard_map/all_to_all | solution.py:39
  195.3 3.2 copy.247
  198.5 2.4 copy.245
  200.9 5.3 %convolution_convert_fusion = bf16[640,1280]{1,0:T(8,128)(2,1)} fusion(bf16[1024,640]{1,0:T(8,128)(2,1)} %bitcast.342, bf16[1,1024,1280]{2,1,0:T(8,128)(2,1)} %all-gather.7.cloned.1.call-done), kind=kOutput, calls=%fused_computation.24 | convolution fusion | flops 1678540800 | bytes 5570560 | tf_op jit(solution)/shard_map/dot_general | solution.py:163
  206.2 20.4 %all-to-all-done.4 = f32[8,40,8,128]{3,2,1,0:T(8,128)} async-done(((f32[8,40,8,128]{3,2,1,0:T(8,128)}), f32[8,40,8,128]{3,2,1,0:T(8,128)}, u32[]{:S(2)}, u32[]{:S(2)}) %all-to-all-start.4) | async-done | bytes 1310752 | tf_op jit(solution)/shard_map/all_to_all | solution.py:39
  226.6 4.5 %all-to-all-start.7 = ((bf16[8,80,1280]{2,1,0:T(8,128)(2,1)}), bf16[8,80,1280]{2,1,0:T(8,128)(2,1)}, u32[]{:S(2)}, u32[]{:S(2)}) async-start(bf16[8,80,1280]{2,1,0:T(8,128)(2,1)} %bitcast.340), calls=%async_computation.7 | async-start | bytes 3276800 | tf_op jit(solution)/shard_map/all_to_all | solution.py:167
  231.1 4.3 %fusion.24 = bf16[1,256,2560]{1,2,0:T(8,128)(2,1)} fusion(f32[1,256,4,640]{1,3,2,0:T(8,128)} %copy.218, f32[1,256,40,64]{1,3,2,0:T(8,128)S(1)} %get-tuple-element.108, f32[256]{0:T(256)S(1)} %get-tuple-element.107, f32[256]{0:T(256)S(1)} %get-tuple-element.106, f32[2560]{0:T(1024)S(1)} %copy-done.25, bf16[1,256,2560]{1,2,0:T(8,128)(2,1)} %copy.229), kind=kLoop, calls=%fused_computation.40 | loop fusion | flops 12451840 | bytes 7876608 | tf_op jit(solution)/shard_map/convert_element_type | solution.py:211
  235.4 2.4 copy.251
  237.9 4.0 fusion.27
  242.6 3.2 copy.231
  245.9 2.4 fusion.99
  248.9 1.7 constant_dynamic-update-slice_fusion.8
  251.3 1.7 constant_dynamic-update-slice_fusion.6
  253.7 1.7 fusion.102
  256.0 13.1 %all-to-all-done.7 = bf16[8,80,1280]{2,1,0:T(8,128)(2,1)} async-done(((bf16[8,80,1280]{2,1,0:T(8,128)(2,1)}), bf16[8,80,1280]{2,1,0:T(8,128)(2,1)}, u32[]{:S(2)}, u32[]{:S(2)}) %all-to-all-start.7) | async-done | bytes 1638432 | tf_op jit(solution)/shard_map/all_to_all | solution.py:167
  269.1 4.3 %all-to-all-start.5 = ((f32[8,40,8,128]{3,2,1,0:T(8,128)}), f32[8,40,8,128]{3,2,1,0:T(8,128)}, u32[]{:S(2)}, u32[]{:S(2)}) async-start(f32[8,40,8,128]{3,2,1,0:T(8,128)} %broadcast_dynamic-update-slice_fusion), calls=%async_computation.5 | async-start | bytes 2621440 | tf_op jit(solution)/shard_map/all_to_all | solution.py:45
  273.5 13.1 %fusion.6 = (f32[40,256]{1,0:T(8,128)}, f32[40,256]{1,0:T(8,128)S(1)}, f32[256,256]{1,0:T(8,128)S(1)}) fusion(f32[40,256]{1,0:T(8,128)} %get-tuple-element.88, f32[256,256]{1,0:T(8,128)S(1)} %copy-done.17, pred[256,256]{1,0:T(8,128)(4,1)} %copy-done.26, f32[256,40,64]{0,2,1:T(8,128)} %bitcast.325, f32[256,40]{0,1:T(8,128)S(1)} %fusion.124, ...), kind=kOutput, calls=%fused_computation.7 | convolution fusion | flops 1030795264 | bytes 5996544 | tf_op jit(solution)/shard_map/transpose(jvp(hcts,cshp->cthp))/dot_general | solution.py:100
  286.6 1.5 copy.239
  288.9 2.2 copy.248
  291.0 4.4 %multiply_reduce_fusion.6 = f32[4,640]{1,0:T(4,128)S(1)} fusion(f32[1,256,4,640]{3,1,2,0:T(8,128)} %copy.248, f32[1,256,4,640]{3,1,2,0:T(8,128)} %copy.247, f32[256]{0:T(256)S(1)} %copy-done.31, f32[4,256,640]{2,1,0:T(8,128)} %copy-done.6), kind=kLoop, calls=%fused_computation.70 | loop fusion | flops 5240320 | bytes 7875584 | tf_op jit(solution)/shard_map/transpose(jvp())/reduce_sum | solution.py:109
  296.1 1.3 fusion.118
  297.4 3.5 fusion.93
  302.1 2.6 convert_reduce_fusion
  304.7 2.1 multiply_reduce_fusion.10
  308.1 3.3 fusion.34
  311.5 7.5 %multiply_reduce_fusion.5 = (f32[40]{0:T(128)}, f32[256,40]{0,1:T(8,128)}, f32[1,256,40,64]{1,3,2,0:T(8,128)}) fusion(f32[1,256,40,64]{1,3,2,0:T(8,128)S(1)} %copy-done.9, f32[1,256,40,64]{1,3,2,0:T(8,128)S(1)} %bitcast.327, f32[256,40]{0,1:T(8,128)S(1)} %fusion.124, f32[256,40]{0,1:T(8,128)S(1)} %get-tuple-element.87, ...), kind=kOutput, calls=%fused_computation.69 | convolution fusion | flops 1019074560 | bytes 10977440 | tf_op jit(solution)/shard_map/transpose(jvp(hcts,cshp->cthp))/dot_general | solution.py:100
  318.9 3.3 copy.235
  322.2 3.7 fusion.88
  325.9 5.4 %multiply_reduce_fusion.4 = (f32[2816]{0:T(1024)S(1)}, f32[2816]{0:T(1024)S(1)}, f32[2816]{0:T(1024)S(1)}, f32[2816]{0:T(1024)S(1)}, f32[2816]{0:T(1024)}, /*index=5*/f32[256,2816]{1,0:T(8,128)S(1)}) fusion(f32[259,2816]{1,0:T(8,128)S(1)} %copy-done.3, f32[256,2816]{1,0:T(8,128)} %get-tuple-element.90, f32[256,2560]{1,0:T(8,128)} %copy.235, ...), kind=kLoop, calls=%fused_computation.32 | loop fusion | flops 15845632 | bytes 22993920 | tf_op jit(solution)/shard_map/transpose(jvp())/reduce_sum | solution.py:70
  333.4 2.5 reduce-window.16
  342.1 1.4 select_maximum_fusion
  343.5 5.1 %all-to-all-start.8 = ((f32[32,1,640]{2,1,0:T(1,128)}), f32[32,1,640]{2,1,0:T(1,128)S(1)}, u32[]{:S(2)}, u32[]{:S(2)}) async-start(f32[32,1,640]{2,1,0:T(1,128)} %bitcast.102), calls=%async_computation.8 | async-start | bytes 163840 | tf_op jit(solution)/shard_map/all_to_all | solution.py:56
  348.6 1.6 broadcast_multiply_fusion.3
  350.3 1.3 collective-permute-start.1
  352.8 3.8 collective-permute-done.1
  357.9 40.0 %all-gather.1 = f32[32,1,640]{2,1,0:T(1,128)S(1)} all-gather(f32[1,1,640]{2,1,0:T(1,128)S(1)} %reshape.1035), channel_id=1, replica_groups=mesh['seq'=8,'dp'=4] {'seq','dp'}, dimensions={0}, use_global_device_ids=true | all-gather | bytes 84480 | tf_op jit(solution)/shard_map/all_gather | solution.py:57
  400.0 3.8 copy.324
  (196 shorter events, 40.6 us)
Async XLA Ops:
  7.2 79.9 %copy-start = (bf16[640,1280]{1,0:T(8,128)(2,1)S(1)}, bf16[640,1280]{1,0:T(8,128)(2,1)}, u32[]{:S(2)}) copy-start(bf16[640,1280]{1,0:T(8,128)(2,1)} %param.20) | copy-start | bytes 4915204
  8.1 16.8 %collective-permute-start = (bf16[3,2816]{1,0:T(4,128)(2,1)S(1)}, bf16[3,2816]{1,0:T(4,128)(2,1)S(1)}, u32[]{:S(2)}, u32[]{:S(2)}) collective-permute-start(bf16[3,2816]{1,0:T(4,128)(2,1)S(1)} %slice_bitcast_fusion), channel_id=1, source_target_pairs={{0,4},{4,8},{8,12},{12,16},{16,20},{20,24},{24,28},{1,5},{5,9},{9,... | collective-permute-start | bytes 50696 | tf_op jit(solution)/shard_map/ppermute | solution.py:21
  13.7 2.4 copy-start.50
  16.2 13.4 %copy-start.20 = (f32[40,1,256]{0,2,1:T(8,128)}, f32[40,1,256]{0,2,1:T(8,128)S(1)}, u32[]{:S(2)}) copy-start(f32[40,1,256]{0,2,1:T(8,128)S(1)} %get-tuple-element.97) | copy-start | bytes 122884
  16.2 10.4 %copy-start.33 = (f32[2816]{0:T(1024)S(1)}, f32[2816]{0:T(1024)}, u32[]{:S(2)}) copy-start(f32[2816]{0:T(1024)} %param.15) | copy-start | bytes 33796
  16.9 23.6 %all-to-all-start.1 = ((f32[8,1,40]{2,1,0:T(1,128)}), f32[8,1,40]{2,1,0:T(1,128)S(1)}, u32[]{:S(2)}, u32[]{:S(2)}) async-start(f32[8,1,40]{2,1,0:T(1,128)} %broadcast_in_dim.32), calls=%async_computation.1 | async-start | bytes 8192 | tf_op jit(solution)/shard_map/all_to_all | solution.py:26
  24.9 4.7 %copy-start.21 = (f32[2816]{0:T(1024)}, f32[2816]{0:T(1024)S(1)}, u32[]{:S(2)}) copy-start(f32[2816]{0:T(1024)S(1)} %get-tuple-element.70) | copy-start | bytes 33796
  24.9 4.7 %copy-start.22 = (f32[2816]{0:T(1024)}, f32[2816]{0:T(1024)S(1)}, u32[]{:S(2)}) copy-start(f32[2816]{0:T(1024)S(1)} %get-tuple-element.71) | copy-start | bytes 33796
  24.9 4.7 %copy-start.23 = (f32[2816]{0:T(1024)}, f32[2816]{0:T(1024)S(1)}, u32[]{:S(2)}) copy-start(f32[2816]{0:T(1024)S(1)} %get-tuple-element.72) | copy-start | bytes 33796
  24.9 4.7 %copy-start.24 = (f32[2816]{0:T(1024)}, f32[2816]{0:T(1024)S(1)}, u32[]{:S(2)}) copy-start(f32[2816]{0:T(1024)S(1)} %get-tuple-element.73) | copy-start | bytes 33796
  26.6 3.0 copy-start.2
  29.6 1.6 copy-start.12
  40.5 0.6 copy-start.32
  41.1 36.8 %all-to-all-start.2 = ((f32[8,40,8,128]{3,2,1,0:T(8,128)}), f32[8,40,8,128]{3,2,1,0:T(8,128)S(1)}, u32[]{:S(2)}, u32[]{:S(2)}) async-start(f32[8,40,8,128]{3,2,1,0:T(8,128)} %copy.225), calls=%async_computation.2 | async-start | bytes 2621440 | tf_op jit(solution)/shard_map/all_to_all | solution.py:39
  47.1 40.0 %all-gather.7.cloned.1.call-start = ((), (), s32[]{:S(2)}) async-start(), calls=%async_computation.10 | async-start | bytes 3276800 | tf_op jit(solution)/shard_map/all_gather | solution.py:154
  49.8 33.6 %copy-start.34 = (f32[40]{0:T(128)}, f32[40]{0:T(128)S(1)}, u32[]{:S(2)}) copy-start(f32[40]{0:T(128)S(1)} %get-tuple-element.100) | copy-start | bytes 484
  49.8 33.6 %copy-start.37 = (f32[40]{0:T(128)}, f32[40]{0:T(128)S(1)}, u32[]{:S(2)}) copy-start(f32[40]{0:T(128)S(1)} %get-tuple-element.102) | copy-start | bytes 484
  49.8 33.6 %copy-start.39 = (f32[40]{0:T(128)}, f32[40]{0:T(128)S(1)}, u32[]{:S(2)}) copy-start(f32[40]{0:T(128)S(1)} %get-tuple-element.101) | copy-start | bytes 484
  49.8 33.6 %copy-start.41 = (f32[40]{0:T(128)}, f32[40]{0:T(128)S(1)}, u32[]{:S(2)}) copy-start(f32[40]{0:T(128)S(1)} %get-tuple-element.103) | copy-start | bytes 484
  49.9 33.6 %copy-start.46 = (f32[40]{0:T(128)}, f32[40]{0:T(128)S(1)}, u32[]{:S(2)}) copy-start(f32[40]{0:T(128)S(1)} %get-tuple-element.99) | copy-start | bytes 484
  49.9 33.6 %copy-start.48 = (f32[40]{0:T(128)}, f32[40]{0:T(128)S(1)}, u32[]{:S(2)}) copy-start(f32[40]{0:T(128)S(1)} %get-tuple-element.104) | copy-start | bytes 484
  83.4 35.0 %all-to-all-start.3 = ((f32[8,40,8,128]{3,2,1,0:T(8,128)}), f32[8,40,8,128]{3,2,1,0:T(8,128)S(1)}, u32[]{:S(2)}, u32[]{:S(2)}) async-start(f32[8,40,8,128]{3,2,1,0:T(8,128)} %fusion.100), calls=%async_computation.3 | async-start | bytes 2621440 | tf_op jit(solution)/shard_map/all_to_all | solution.py:45
  118.4 1.1 copy-start.10
  118.4 5.2 %copy-start.25 = (f32[2560]{0:T(1024)S(1)}, f32[2560]{0:T(1024)}, u32[]{:S(2)}) copy-start(f32[2560]{0:T(1024)} %param.19) | copy-start | bytes 30724
  119.5 35.4 %all-to-all-start = ((f32[4,256,640]{2,1,0:T(8,128)}), f32[4,256,640]{2,1,0:T(8,128)S(1)}, u32[]{:S(2)}, u32[]{:S(2)}) async-start(f32[4,256,640]{2,1,0:T(8,128)} %bitcast.338), calls=%async_computation | async-start | bytes 5242880 | tf_op jit(solution)/shard_map/all_to_all | solution.py:159
  123.8 54.2 %copy-start.14 = (f32[256,40]{0,1:T(8,128)}, f32[256,40]{0,1:T(8,128)S(1)}, u32[]{:S(2)}) copy-start(f32[256,40]{0,1:T(8,128)S(1)} %copy.227) | copy-start | bytes 122884
  126.2 4.5 %copy-start.11 = (f32[8,40,8,128]{3,2,1,0:T(8,128)S(1)}, f32[8,40,8,128]{3,2,1,0:T(8,128)}, u32[]{:S(2)}) copy-start(f32[8,40,8,128]{3,2,1,0:T(8,128)} %copy-done.10) | copy-start | bytes 3932164
  129.4 27.9 %copy-start.26 = (pred[256,256]{1,0:T(8,128)(4,1)}, pred[256,256]{1,0:T(8,128)(4,1)S(1)}, u32[]{:S(2)}) copy-start(pred[256,256]{1,0:T(8,128)(4,1)S(1)} %iota_compare_fusion) | copy-start | bytes 196612
  130.7 26.6 %copy-start.16 = (f32[256,256]{1,0:T(8,128)}, f32[256,256]{1,0:T(8,128)S(1)}, u32[]{:S(2)}) copy-start(f32[256,256]{1,0:T(8,128)S(1)} %fusion.115) | copy-start | bytes 786436
  154.8 2.5 copy-start.6
  154.8 2.5 copy-start.28
  154.8 2.5 copy-start.51
  157.3 10.1 %copy-start.4 = (f32[1,256,2560]{1,2,0:T(8,128)S(1)}, f32[1,256,2560]{1,2,0:T(8,128)}, u32[]{:S(2)}) copy-start(f32[1,256,2560]{1,2,0:T(8,128)} %convert_element_type.89) | copy-start | bytes 7864324
  167.4 70.4 %copy-start.30 = (f32[256]{0:T(256)}, f32[256]{0:T(256)S(1)}, u32[]{:S(2)}) copy-start(f32[256]{0:T(256)S(1)} %get-tuple-element.106) | copy-start | bytes 3076
  169.4 21.6 %all-to-all-start.6 = ((bf16[256,4,640]{0,2,1:T(8,128)(2,1)}), bf16[256,4,640]{0,2,1:T(8,128)(2,1)}, u32[]{:S(2)}, u32[]{:S(2)}) async-start(bf16[256,4,640]{0,2,1:T(8,128)(2,1)} %multiply_convert_fusion), calls=%async_computation.6 | async-start | bytes 2621440 | tf_op jit(solution)/shard_map/all_to_all | solution.py:162
  177.9 1.6 copy-start.7
  191.0 35.6 %all-to-all-start.4 = ((f32[8,40,8,128]{3,2,1,0:T(8,128)}), f32[8,40,8,128]{3,2,1,0:T(8,128)}, u32[]{:S(2)}, u32[]{:S(2)}) async-start(f32[8,40,8,128]{3,2,1,0:T(8,128)} %copy.232), calls=%async_computation.4 | async-start | bytes 2621440 | tf_op jit(solution)/shard_map/all_to_all | solution.py:39
  226.6 42.5 %all-to-all-start.7 = ((bf16[8,80,1280]{2,1,0:T(8,128)(2,1)}), bf16[8,80,1280]{2,1,0:T(8,128)(2,1)}, u32[]{:S(2)}, u32[]{:S(2)}) async-start(bf16[8,80,1280]{2,1,0:T(8,128)(2,1)} %bitcast.340), calls=%async_computation.7 | async-start | bytes 3276800 | tf_op jit(solution)/shard_map/all_to_all | solution.py:167
  242.6 3.3 copy-start.35
  242.6 3.3 copy-start.38
  242.6 3.3 copy-start.40
  242.6 3.3 copy-start.42
  242.6 3.3 copy-start.44
  242.6 3.3 copy-start.47
  242.6 3.3 copy-start.49
  245.8 5.5 %copy-start.36 = (f32[40]{0:T(128)S(1)}, f32[40]{0:T(128)}, u32[]{:S(2)}) copy-start(f32[40]{0:T(128)} %copy-done.34) | copy-start | bytes 484
  245.8 7.8 %copy-start.45 = (f32[40]{0:T(128)S(1)}, f32[40]{0:T(128)}, u32[]{:S(2)}) copy-start(f32[40]{0:T(128)} %get-tuple-element.98) | copy-start | bytes 484
  248.3 25.2 %copy-start.17 = (f32[256,256]{1,0:T(8,128)S(1)}, f32[256,256]{1,0:T(8,128)}, u32[]{:S(2)}) copy-start(f32[256,256]{1,0:T(8,128)} %copy-done.16) | copy-start | bytes 786436
  269.1 35.6 %all-to-all-start.5 = ((f32[8,40,8,128]{3,2,1,0:T(8,128)}), f32[8,40,8,128]{3,2,1,0:T(8,128)}, u32[]{:S(2)}, u32[]{:S(2)}) async-start(f32[8,40,8,128]{3,2,1,0:T(8,128)} %broadcast_dynamic-update-slice_fusion), calls=%async_computation.5 | async-start | bytes 2621440 | tf_op jit(solution)/shard_map/all_to_all | solution.py:45
  273.4 126.6 %all-gather.5.cloned.1.call-start = ((), (), s32[]{:S(2)}) async-start(), calls=%async_computation.9 | async-start | bytes 3686400 | tf_op jit(solution)/shard_map/all_gather | solution.py:175
  288.9 2.2 copy-start.31
  291.0 6.3 %copy-start.8 = (f32[1,256,40,64]{1,3,2,0:T(8,128)S(1)}, f32[1,256,40,64]{1,3,2,0:T(8,128)}, u32[]{:S(2)}) copy-start(f32[1,256,40,64]{1,3,2,0:T(8,128)} %copy-done.7) | copy-start | bytes 7864324
  291.0 6.3 %copy-start.15 = (f32[256,40]{0,1:T(8,128)S(1)}, f32[256,40]{0,1:T(8,128)}, u32[]{:S(2)}) copy-start(f32[256,40]{0,1:T(8,128)} %copy-done.14) | copy-start | bytes 122884
  302.1 6.0 %copy-start.5 = (f32[256,2560]{0,1:T(8,128)S(1)}, f32[256,2560]{0,1:T(8,128)}, u32[]{:S(2)}) copy-start(f32[256,2560]{0,1:T(8,128)} %copy.219) | copy-start | bytes 7864324
  308.1 3.4 copy-start.9
  308.1 3.4 copy-start.18
  308.1 3.4 copy-start.27
  308.1 3.3 copy-start.29
  322.2 3.7 copy-start.3
  325.9 5.5 %copy-start.19 = (f32[256,40]{0,1:T(8,128)S(1)}, f32[256,40]{0,1:T(8,128)}, u32[]{:S(2)}) copy-start(f32[256,40]{0,1:T(8,128)} %get-tuple-element.109) | copy-start | bytes 122884
  325.9 11.2 %copy-start.13 = (f32[1,40,256]{2,1,0:T(8,128)S(1)}, f32[1,40,256]{2,1,0:T(8,128)}, u32[]{:S(2)}) copy-start(f32[1,40,256]{2,1,0:T(8,128)} %param.13) | copy-start | bytes 122884
  343.5 14.4 %all-to-all-start.8 = ((f32[32,1,640]{2,1,0:T(1,128)}), f32[32,1,640]{2,1,0:T(1,128)S(1)}, u32[]{:S(2)}, u32[]{:S(2)}) async-start(f32[32,1,640]{2,1,0:T(1,128)} %bitcast.102), calls=%async_computation.8 | async-start | bytes 163840 | tf_op jit(solution)/shard_map/all_to_all | solution.py:56
  350.3 6.3 %collective-permute-start.1 = (f32[3,2816]{1,0:T(4,128)S(1)}, f32[3,2816]{1,0:T(4,128)S(1)}, u32[]{:S(2)}, u32[]{:S(2)}) collective-permute-start(f32[3,2816]{1,0:T(4,128)S(1)} %pad_add_fusion.1), channel_id=1, source_target_pairs={{4,0},{8,4},{12,8},{16,12},{20,16},{24,20},{28,24},{5,1},{9,5},{13... | collective-permute-start | bytes 101384 | tf_op jit(solution)/shard_map/ppermute | solution.py:21
  399.4 4.5 %copy-start.1 = (bf16[640,1280]{1,0:T(8,128)(2,1)S(1)}, bf16[640,1280]{1,0:T(8,128)(2,1)}, u32[]{:S(2)}) copy-start(bf16[640,1280]{1,0:T(8,128)(2,1)} %param.20) | copy-start | bytes 4915204
  (1 other events, 0.5 us)
Sparse Core Ops, SparseCore 0:
  49.4 26.9 all-gather.6
  304.8 62.9 all-gather.4
